TPU v7x, 32 devices: a whole 2x2x4 slice. The times are simulated.
32 devices in a mesh: groups: 2 (over y), seq: 8 (over z, x), head: 2 (over core).
Axes of the slice: x: 2, y: 2, z: 4, core: 2. Of those that a mesh axis runs over, the one named last changes fastest.
Arguments:
- queries: bfloat16 [2048, 1024], P(('groups', 'seq'), 'head'), parts along dimension 0, may hold values from -6 to 6
- key_rows: bfloat16 [2048, 2, 1024], P(('groups', 'seq'), None, 'head'), parts along dimension 0, may hold values from -6 to 6
- value_rows: bfloat16 [2048, 2, 1024], P(('groups', 'seq'), None, 'head'), parts along dimension 0, may hold values from -6 to 6
- strengths: float32 [8, 2, 2048], P('head', None, ('groups', 'seq')), parts along dimension 2, may hold values from 0.2 to 2, as said below
- log_gate: float32 [8, 2048], P('head', ('groups', 'seq')), parts along dimension 1, may hold values from -1.2 to 0, as said below
- keep_flag: int32 [2048], P(('groups', 'seq')), parts along dimension 0, may hold values 0 or 1
- norm_gain: float32 [1024], P('head'), may hold values from 0.1 to 1.9
- out_weight: bfloat16 [1024, 2048], P('head'), may hold values from -0.1875 to 0.1875
Outputs:
- projected: bfloat16 [2048, 2048], P(('groups', 'seq', 'head')), parts along dimension 0
There are 2 independent parts, one for each index of `groups`. A program takes and returns all parts, laid end to end along the dimension named above; an argument that names none is the same for every part. Nothing has to cross between parts.
Inputs may be any that keep to these rules, and one draw needn't show every extreme that they name: `strengths`: reflection strength of each head, key and token. `log_gate`: logarithm of each head's decay at each token.
All inputs are finite; a program needn't handle non-finite values. No bound on the sum of `keep_flag` on one device may be relied on, other than what follows from the above.
Results may differ from a plain program's by a relative error of at most 0.0049.
Values may be sent and summed in bfloat16 or wider, within the bound.
A program may use at most 64 MiB of HBM per device.

v0:
```python
import jax
import jax.numpy as jnp
from jax import lax
from jax.sharding import PartitionSpec as P

DK = 128
DV = 128
BLOCK = 64


def swapped(value, axis, bit):
    return lax.ppermute(value, axis, [(i, i ^ 1 << bit) for i in range(lax.axis_size(axis))])


def unit_rows(values_in):
    return values_in * lax.rsqrt(jnp.sum(values_in * values_in, axis=-1, keepdims=True) + 1e-06)


def block_pieces(q_unit, k_unit, v_rows, beta_eff, step_log):
    highest = lax.Precision.HIGHEST
    size = k_unit.shape[-2]
    key_width = k_unit.shape[-1]
    query_count = q_unit.shape[-2]
    cum_log = jnp.cumsum(step_log, axis=-1)
    sequence_indices = jnp.arange(size)
    strict_lower = sequence_indices[:, None] > sequence_indices[None, :]
    lower_incl = sequence_indices[:, None] >= sequence_indices[None, :]
    log_gap = cum_log[..., :, None] - cum_log[..., None, :]
    decay_pair = jnp.where(lower_incl, jnp.exp(jnp.where(lower_incl, log_gap, 0.0)), 0.0)
    key_gram = jnp.einsum("...id,...jd->...ij", k_unit, k_unit, precision=highest)
    lower_part = jnp.where(strict_lower, beta_eff[..., :, None] * decay_pair * key_gram, 0.0)
    system = lower_part + jnp.eye(size, dtype=k_unit.dtype)
    both_sides = jnp.concatenate(
        [(beta_eff * jnp.exp(cum_log))[..., None] * k_unit, beta_eff[..., None] * v_rows], axis=-1
    )
    solved = jax.scipy.linalg.solve_triangular(system, both_sides, lower=True, unit_diagonal=True)
    wide_w = solved[..., :key_width]
    wide_u = solved[..., key_width:]
    last_log = cum_log[..., -1:]
    to_end = jnp.exp(last_log - cum_log)
    faded_keys = k_unit * to_end[..., None]
    eye_keys = jnp.eye(key_width, dtype=k_unit.dtype)
    block_trans = jnp.exp(last_log)[..., None] * eye_keys - jnp.einsum(
        "...ld,...le->...de", faded_keys, wide_w, precision=highest
    )
    block_bias = jnp.einsum("...ld,...le->...de", faded_keys, wide_u, precision=highest)
    query_log = cum_log[..., 1::2]
    query_pos = 2 * jnp.arange(query_count) + 1
    visible = query_pos[:, None] >= sequence_indices[None, :]
    query_gap = query_log[..., :, None] - cum_log[..., None, :]
    query_decay = jnp.where(visible, jnp.exp(jnp.where(visible, query_gap, 0.0)), 0.0)
    query_mix = query_decay * jnp.einsum("...td,...ld->...tl", q_unit, k_unit, precision=highest)
    local_out = jnp.einsum("...tl,...le->...te", query_mix, wide_u, precision=highest)
    reach_query = jnp.exp(query_log)[..., None] * q_unit - jnp.einsum(
        "...tl,...ld->...td", query_mix, wide_w, precision=highest
    )
    return (local_out, reach_query, block_trans, block_bias)


def batch_mm(left_mat, right_mat):
    return jnp.einsum("hij,hjk->hik", left_mat, right_mat, precision=lax.Precision.HIGHEST)


def compose_stack(earlier, later):
    later_trans = later[..., :DK]
    added = jnp.concatenate([jnp.zeros_like(later_trans), later[..., DK:]], axis=-1)
    return batch_mm(later_trans, earlier) + added


def paired_prefix(total_map, identity_map):
    seq_rank = lax.axis_index("seq")
    levels = lax.axis_size("seq").bit_length() - 1
    running = total_map
    before = identity_map
    for bit_pos in range(levels):
        partner = swapped(running, "seq", bit_pos)
        is_upper = seq_rank // 2**bit_pos % 2 == 1
        earlier_part = jnp.where(is_upper, partner, running)
        later_part = jnp.where(is_upper, running, partner)
        shifted = compose_stack(partner, before)
        before = jnp.where(is_upper, shifted, before)
        running = compose_stack(earlier_part, later_part)
    return before


def shards(queries, key_rows, value_rows, strengths, log_gate, keep_flag, norm_gain, out_weight):
    tok_rows = queries.shape[0]
    head_count = strengths.shape[0]
    blocks = tok_rows // BLOCK
    q_unit = unit_rows(queries.astype(jnp.float32).reshape(tok_rows, head_count, DK))
    q_unit = q_unit.transpose(1, 0, 2).reshape(head_count, blocks, BLOCK, DK)
    k_unit = unit_rows(key_rows.astype(jnp.float32).reshape(tok_rows, 2, head_count, DK))
    k_unit = k_unit.transpose(2, 0, 1, 3).reshape(head_count, blocks, 2 * BLOCK, DK)
    v_rows = value_rows.astype(jnp.float32).reshape(tok_rows, 2, head_count, DV)
    v_rows = v_rows.transpose(2, 0, 1, 3).reshape(head_count, blocks, 2 * BLOCK, DV)
    live_flag = keep_flag.astype(jnp.float32)
    beta_eff = (
        (strengths * live_flag[None, None, :])
        .transpose(0, 2, 1)
        .reshape(head_count, blocks, 2 * BLOCK)
    )
    first_log = log_gate * live_flag[None, :]
    step_log = jnp.stack([first_log, jnp.zeros_like(first_log)], axis=-1).reshape(
        head_count, blocks, 2 * BLOCK
    )
    local_out, reach_query, block_trans, block_bias = block_pieces(
        q_unit, k_unit, v_rows, beta_eff, step_log
    )
    block_maps = jnp.concatenate([block_trans, block_bias], axis=-1).swapaxes(0, 1)
    eye_heads = jnp.broadcast_to(jnp.eye(DK, dtype=jnp.float32), (head_count, DK, DK))
    identity_map = jnp.concatenate(
        [eye_heads, jnp.zeros((head_count, DK, DV), jnp.float32)], axis=-1
    )

    def compose_block(carry_map, block_map):
        return (compose_stack(carry_map, block_map), carry_map)

    total_map, enter_maps = lax.scan(compose_block, identity_map, block_maps)
    prefix_map = paired_prefix(total_map, identity_map)
    incoming = prefix_map[..., DK:]

    def replay(state_now, pieces):
        reach_block, local_block, map_block = pieces
        out_rows = local_block + batch_mm(reach_block, state_now)
        state_next = batch_mm(map_block[..., :DK], state_now) + map_block[..., DK:]
        return (state_next, out_rows)

    _, block_outs = lax.scan(
        replay, incoming, (reach_query.swapaxes(0, 1), local_out.swapaxes(0, 1), block_maps)
    )
    attended = block_outs.swapaxes(0, 1)
    attended = attended.reshape(head_count, tok_rows, DV)
    inv_rms = lax.rsqrt(jnp.mean(attended * attended, axis=-1, keepdims=True) + 1e-05)
    gain_rows = norm_gain.reshape(head_count, DV)[:, None, :]
    normed = (
        (attended * inv_rms * gain_rows)
        .transpose(1, 0, 2)
        .reshape(tok_rows, head_count * DV)
        .astype(jnp.bfloat16)
    )
    projected = lax.psum_scatter(
        jnp.dot(normed, out_weight, preferred_element_type=jnp.float32),
        "head",
        scatter_dimension=0,
        tiled=True,
    )
    return projected.astype(jnp.bfloat16)


def solution(mesh):
    in_specs = (
        P(("groups", "seq"), "head"),
        P(("groups", "seq"), None, "head"),
        P(("groups", "seq"), None, "head"),
        P("head", None, ("groups", "seq")),
        P("head", ("groups", "seq")),
        P(("groups", "seq")),
        P("head"),
        P("head", None),
    )
    out_specs = P(("groups", "seq", "head"), None)
    return jax.shard_map(shards, mesh=mesh, in_specs=in_specs, out_specs=out_specs, check_vma=False)
```

profile of v0, /device:TPU:31, one launch (start us, length us, event | category | flops | bytes accessed | tf_op | source)
XLA Modules:
  0.0 194.2 jit_solution(2969645522171671114)
XLA Ops:
  9.0 1.2 reduce_window_sum.11
  11.5 1.2 reshape.118
  14.0 2.1 %fusion.11 = f32[4,2,1,128,128]{4,3,2,1,0:T(8,128)} fusion(f32[4,2,128,128]{3,2,1,0:T(8,128)S(1)} %bitcast.100, f32[128,128]{1,0:T(8,128)S(1)} %fusion.42, f32[4,2,128]{2,1,0:T(2,128)S(1)} %reduce_window_sum.11, f32[4,2,128]{2,1,0:T(2,128)S(1)} %copy.79, f32[128,128]{1,0:T(8,128)S(1)} %get-tuple-element.115, pred[128,128]{1,0:T(8,128)(4,1)S(1)} %get-tuple-element.112, ...), kind=kOutput, calls=%fused_computation.19 | convolution fusion | flops 202506240 | bytes 1236992 | tf_op jit(solution)/shard_map/...id,...jd->...ij/dot_general | solution.py:30
  16.0 80.0 %custom-call.4 = f32[4,2,1,128,128]{3,4,2,1,0:T(8,128)} custom-call(f32[4,2,1,128,128]{4,3,2,1,0:T(8,128)} %fusion.11), custom_call_target="InvertDiagBlocksLowerTriangular" | custom-call | tf_op jit(solution)/shard_map/jit(_solve_triangular)/vmap(vmap())/triangular_solve | solution.py:36
  98.5 1.2 fusion.22
  99.7 1.2 convolution_subtract_fusion
  101.1 5.1 %while.22 = (s32[]{:T(128)}, f32[4,128,256]{2,1,0:T(8,128)}, f32[2,4,128,256]{3,2,1,0:T(8,128)S(1)}, s32[]{:T(128)}) while((s32[]{:T(128)}, f32[4,128,256]{2,1,0:T(8,128)}, f32[2,4,128,256]{3,2,1,0:T(8,128)S(1)}, s32[]{:T(128)}) %tuple.43), condition=%wide.region_3.4_spmd, body=%wide.region_2.0_spmd.sunk | while | flops 201457664 | bytes 4194369 | solution.py:118
  102.2 1.4 convolution_add_fusion.8
  104.7 1.4 convolution_add_fusion.8
  107.2 1.2 multiply_reduce_fusion.1
  108.4 1.9 multiply_bitcast_fusion.1
  110.3 8.9 %collective-permute-done = f32[4,128,256]{2,1,0:T(8,128)} collective-permute-done((f32[4,128,256]{2,1,0:T(8,128)}, f32[4,128,256]{2,1,0:T(8,128)}, u32[]{:S(2)}, u32[]{:S(2)}) %collective-permute-start) | collective-permute-done | bytes 524320 | tf_op jit(solution)/shard_map/ppermute | solution.py:12
  119.2 1.1 broadcast_select_fusion
  120.4 2.5 %convolution_add_fusion.5 = f32[4,128,256]{2,1,0:T(8,128)} fusion(f32[4,128,128]{2,1,0:T(8,128)S(1)} %slice.79, f32[4,128,256]{2,1,0:T(8,128)} %collective-permute-done, f32[4,128,256]{2,1,0:T(8,128)S(1)} %copy-done.1, f32[4,128,256]{2,1,0:T(8,128)S(1)} %broadcast_select_fusion, pred[]{:T(512)S(6)} %eq.30), kind=kOutput, calls=%fused_computation.23 | convolution fusion | flops 201588736 | bytes 2097153 | tf_op jit(solution)/shard_map/hij,hjk->hik/dot_general | solution.py:61
  124.3 2.2 %convolution_multiply_fusion.1 = f32[4,2,64,128]{3,2,1,0:T(8,128)S(1)} fusion(f32[4,2,64,128]{3,2,1,0:T(8,128)S(1)} %bitcast.105, f32[4,2,128,128]{3,2,1,0:T(8,128)} %bitcast.104, f32[4,2,128]{2,1,0:T(2,128)S(1)} %reduce_window_sum.11, f32[4,2,64]{2,1,0:T(2,128)S(1)} %slice.69, pred[64,128]{1,0:T(8,128)(4,1)S(1)} %iota_compare_fusion.5), kind=kOutput, calls=%fused_computation.27 | convolution fusion | flops 100925440 | bytes 1062912 | tf_op jit(solution)/shard_map/...td,...ld->...tl/dot_general | solution.py:52
  126.5 2.3 %fusion.13 = f32[2,4,64,128]{3,2,0,1:T(8,128)} fusion(f32[4,2,64,128]{3,2,1,0:T(8,128)S(1)} %convolution_multiply_fusion.1, f32[4,2,128,256]{3,2,1,0:T(8,128)} %copy-done.3, f32[4,2,64,128]{3,2,1,0:T(8,128)S(1)} %bitcast.106, f32[4,2,64]{2,1,0:T(2,128)S(1)} %exp.31), kind=kOutput, calls=%fused_computation.25 | convolution fusion | flops 100794368 | bytes 1312768 | tf_op jit(solution)/shard_map/...tl,...ld->...td/dot_general | solution.py:54
  128.8 6.2 %collective-permute-done.1 = f32[4,128,256]{2,1,0:T(8,128)} collective-permute-done((f32[4,128,256]{2,1,0:T(8,128)}, f32[4,128,256]{2,1,0:T(8,128)}, u32[]{:S(2)}, u32[]{:S(2)}) %collective-permute-start.1) | collective-permute-done | bytes 524320 | tf_op jit(solution)/shard_map/ppermute | solution.py:12
  135.1 1.1 broadcast_select_fusion.1
  136.2 2.5 %convolution_add_fusion.3 = f32[4,128,256]{2,1,0:T(8,128)} fusion(f32[4,128,128]{2,1,0:T(8,128)S(1)} %slice.83, f32[4,128,256]{2,1,0:T(8,128)} %collective-permute-done.1, f32[4,128,256]{2,1,0:T(8,128)} %convolution_add_fusion.5, f32[4,128,256]{2,1,0:T(8,128)S(1)} %broadcast_select_fusion.1, pred[]{:T(512)S(6)} %eq.29), kind=kOutput, calls=%fused_computation.20 | convolution fusion | flops 201588736 | bytes 2097153 | tf_op jit(solution)/shard_map/hij,hjk->hik/dot_general | solution.py:61
  138.8 1.3 convolution_bitcast_fusion
  140.1 1.6 convolution_select_fusion
  141.7 1.6 fusion.12
  143.4 21.5 %collective-permute-done.2 = f32[4,128,256]{2,1,0:T(8,128)} collective-permute-done((f32[4,128,256]{2,1,0:T(8,128)}, f32[4,128,256]{2,1,0:T(8,128)}, u32[]{:S(2)}, u32[]{:S(2)}) %collective-permute-start.2) | collective-permute-done | bytes 524320 | tf_op jit(solution)/shard_map/ppermute | solution.py:12
  164.9 1.6 fusion.30
  166.6 5.0 %while.23 = (s32[]{:T(128)}, f32[4,128,128]{2,1,0:T(8,128)S(1)}, f32[2,4,64,128]{3,2,0,1:T(8,128)}, f32[2,4,128,256]{3,2,1,0:T(8,128)S(1)}, f32[2,4,64,128]{3,2,...) while((s32[]{:T(128)}, f32[4,128,128]{2,1,0:T(8,128)S(1)}, f32[2,4,64,128]{3,2,0,1:T(8,128)}, ...), condition=%wide.region_6.7_spmd, body=%wide.region_5.6_spmd.sunk | while | flops 151093248 | bytes 3277913 | solution.py:128
  166.6 2.0 %fusion.73 = f32[2,4,64,128]{3,2,0,1:T(8,128)} fusion(f32[2,4,64,128]{3,2,0,1:T(8,128)} %get-tuple-element.195, s32[]{:T(128)S(6)} %copy.127, f32[4,128,128]{2,1,0:T(8,128)S(1)} %copy.138, f32[2,4,64,128]{3,2,0,1:T(8,128)} %get-tuple-element.205, f32[2,4,64,128]{3,2,0,1:T(8,128)} %get-tuple-element.204), kind=kOutput, calls=%fused_computation.6.clone.1 | convolution fusion | flops 50364416 | bytes 656384 | tf_op jit(solution)/shard_map/while/body/eval_jaxpr/hij,hjk->hik/dot_general | solution.py:61
  169.1 2.0 %fusion.73 = f32[2,4,64,128]{3,2,0,1:T(8,128)} fusion(f32[2,4,64,128]{3,2,0,1:T(8,128)} %get-tuple-element.195, s32[]{:T(128)S(6)} %copy.127, f32[4,128,128]{2,1,0:T(8,128)S(1)} %copy.138, f32[2,4,64,128]{3,2,0,1:T(8,128)} %get-tuple-element.205, f32[2,4,64,128]{3,2,0,1:T(8,128)} %get-tuple-element.204), kind=kOutput, calls=%fused_computation.6.clone.1 | convolution fusion | flops 50364416 | bytes 656384 | tf_op jit(solution)/shard_map/while/body/eval_jaxpr/hij,hjk->hik/dot_general | solution.py:61
  171.5 1.1 fusion.36
  172.7 1.1 fusion.35
  174.0 1.4 fusion.44
  175.4 10.1 %reduce-scatter.2.cloned.1.call-done = f32[64,2048]{1,0:T(8,128)} async-done(((f32[128,2048]{1,0:T(8,128)}), f32[64,2048]{1,0:T(8,128)}) %reduce-scatter.2.cloned.1.call-update) | async-done | bytes 524304 | tf_op jit(solution)/shard_map/reduce_scatter | solution.py:141
  185.6 1.8 convert_element_type.38
  (82 shorter events, 13.5 us)
Async XLA Ops:
  6.5 167.4 %copy-start = (bf16[512,2048]{1,0:T(8,128)(2,1)S(1)}, bf16[512,2048]{1,0:T(8,128)(2,1)}, u32[]{:S(2)}) copy-start(bf16[512,2048]{1,0:T(8,128)(2,1)} %param.19) | copy-start | bytes 6291460
  6.5 179.0 %reduce-scatter.2.cloned.1.call-start = ((), (), s32[]{:S(2)}) async-start(), calls=%async_computation.1 | async-start | bytes 1572864 | tf_op jit(solution)/shard_map/reduce_scatter | solution.py:141
  13.9 85.9 %copy-start.2 = (f32[4,128,2,128]{3,2,1,0:T(2,128)}, f32[4,128,2,128]{3,2,1,0:T(2,128)S(1)}, u32[]{:S(2)}) copy-start(f32[4,128,2,128]{3,2,1,0:T(2,128)S(1)} %copy.76) | copy-start | bytes 1572868
  13.9 83.1 %copy-start.6 = (bf16[128,2,512]{2,1,0:T(2,128)(2,1)S(1)}, bf16[128,2,512]{2,1,0:T(2,128)(2,1)}, u32[]{:S(2)}) copy-start(bf16[128,2,512]{2,1,0:T(2,128)(2,1)} %param.14) | copy-start | bytes 786436
  96.1 1.4 copy-start.5
  97.5 2.2 %copy-start.8 = (f32[4,2]{1,0:T(4,128)S(1)}, f32[4,2]{1,0:T(4,128)}, u32[]{:S(2)}) copy-start(f32[4,2]{1,0:T(4,128)} %copy.75) | copy-start | bytes 100
  98.5 2.4 %copy-start.3 = (f32[4,2,128,256]{3,2,1,0:T(8,128)}, f32[4,2,128,256]{3,2,1,0:T(8,128)S(1)}, u32[]{:S(2)}) copy-start(f32[4,2,128,256]{3,2,1,0:T(8,128)S(1)} %fusion.14) | copy-start | bytes 3145732
  101.1 5.3 %copy-start.7 = (bf16[128,512]{1,0:T(8,128)(2,1)S(1)}, bf16[128,512]{1,0:T(8,128)(2,1)}, u32[]{:S(2)}) copy-start(bf16[128,512]{1,0:T(8,128)(2,1)} %param.12) | copy-start | bytes 393220
  106.1 13.1 %collective-permute-start = (f32[4,128,256]{2,1,0:T(8,128)}, f32[4,128,256]{2,1,0:T(8,128)}, u32[]{:S(2)}, u32[]{:S(2)}) collective-permute-start(f32[4,128,256]{2,1,0:T(8,128)} %get-tuple-element.54), channel_id=1, source_target_pairs={{0,2},{2,0},{4,6},{6,4},{8,10},{10,8},{12,14},{14,12},{1,3},{3,1},... | collective-permute-start | bytes 1572872 | tf_op jit(solution)/shard_map/ppermute | solution.py:12
  107.2 13.2 %copy-start.1 = (f32[4,128,256]{2,1,0:T(8,128)S(1)}, f32[4,128,256]{2,1,0:T(8,128)}, u32[]{:S(2)}) copy-start(f32[4,128,256]{2,1,0:T(8,128)} %get-tuple-element.54) | copy-start | bytes 1572868
  122.9 12.2 %collective-permute-start.1 = (f32[4,128,256]{2,1,0:T(8,128)}, f32[4,128,256]{2,1,0:T(8,128)}, u32[]{:S(2)}, u32[]{:S(2)}) collective-permute-start(f32[4,128,256]{2,1,0:T(8,128)} %convolution_add_fusion.5), channel_id=1, source_target_pairs={{0,4},{2,6},{4,0},{6,2},{8,12},{10,14},{12,8},{14,10},{1,5},{3,7},... | collective-permute-start | bytes 1572872 | tf_op jit(solution)/shard_map/ppermute | solution.py:12
  128.8 10.0 %copy-start.4 = (f32[4,2,128,256]{3,2,1,0:T(8,128)S(1)}, f32[4,2,128,256]{3,2,1,0:T(8,128)}, u32[]{:S(2)}) copy-start(f32[4,2,128,256]{3,2,1,0:T(8,128)} %copy-done.3) | copy-start | bytes 3145732
  138.7 26.2 %collective-permute-start.2 = (f32[4,128,256]{2,1,0:T(8,128)}, f32[4,128,256]{2,1,0:T(8,128)}, u32[]{:S(2)}, u32[]{:S(2)}) collective-permute-start(f32[4,128,256]{2,1,0:T(8,128)} %convolution_add_fusion.3), channel_id=1, source_target_pairs={{0,8},{2,10},{4,12},{6,14},{8,0},{10,2},{12,4},{14,6},{1,9},{3,11}... | collective-permute-start | bytes 1572872 | tf_op jit(solution)/shard_map/ppermute | solution.py:12
  166.6 6.2 %copy-start.9 = (f32[512]{0:T(512)S(1)}, f32[512]{0:T(512)}, u32[]{:S(2)}) copy-start(f32[512]{0:T(512)} %param.18) | copy-start | bytes 6148
Sparse Core Ops, SparseCore 0:
  175.6 9.9 reduce-scatter.1
where the time goes:
time: 196 us; the launch traced here: 194 us
  other arithmetic  94.5 us (48%)
  waiting for transfers between devices  46.8 us (24%)
  matrix products  30.1 us (15%)
  between operations  13.8 us (7%)
  local copies, waits for them, and re-layouts  8.42 us (4%)
    another operation x4, other arithmetic, block_pieces(): jax.scipy.linalg.solve_triangular(system, both_sides, lower=True, unit_di...  80.1 us
    ppermute x3, waiting for transfers between devices, swapped(): lax.ppermute(value, axis, [(i, i ^ 1 << bit) for i in range(lax.axis_size...  36.7 us
    dot_general x11, matrix products, batch_mm(): jnp.einsum('hij,hjk->hik', left_mat, right_mat, precision=lax.Precision.H...  17.4 us
    reduce_scatter x1, waiting for transfers between devices, shards(): lax.psum_scatter(jnp.dot(normed, out_weight, preferred_element_type=jnp.f...  10.1 us
  transfers between devices with their start and end apart: 4, of which 4 were waited for; matrix products, arithmetic and copies ran while one was open for 7% of the time, Pallas kernels for 0%

commit v1 on v0

v1 whole, which is shorter than its diff:
```python
import functools

import jax
import jax.numpy as jnp
from jax import lax
from jax.experimental import pallas as pl
from jax.experimental.pallas import tpu as pltpu
from jax.sharding import PartitionSpec as P

DK = 128
DV = 128
F32 = jnp.float32
BF16 = jnp.bfloat16


def swapped(value, axis, bit):
    return lax.ppermute(value, axis, [(i, i ^ 1 << bit) for i in range(lax.axis_size(axis))])


def split2(x):
    hi = x.astype(BF16)
    return hi, (x - hi.astype(F32)).astype(BF16)


def dot1(a, b):
    return jnp.dot(a, b, preferred_element_type=F32)


def mm3(a, b):
    return dot1(a[0], b[0]) + (dot1(a[0], b[1]) + dot1(a[1], b[0]))


def dot_nt(a, b):
    return lax.dot_general(a, b, (((1,), (1,)), ((), ())), preferred_element_type=F32)


def local_kernel(heads, q_ref, k_ref, v_ref, small_ref, maps_ref, reads_ref, a_sc, xh_sc, xl_sc):
    tok = q_ref.shape[0]
    size = 2 * tok
    width = heads * DK
    row_t = lax.broadcasted_iota(jnp.int32, (tok, tok), 0)
    col_t = lax.broadcasted_iota(jnp.int32, (tok, tok), 1)
    incl = row_t >= col_t
    strict = row_t > col_t
    small = small_ref[...]
    s1 = small.astype(BF16)
    rest = small - s1.astype(F32)
    s2 = rest.astype(BF16)
    s3 = (rest - s2.astype(F32)).astype(BF16)
    upper = jnp.where(row_t <= col_t, 1.0, 0.0).astype(BF16)
    cum = dot1(s1, upper) + (dot1(s2, upper) + dot1(s3, upper))
    srows = small.shape[0]
    cols = jnp.concatenate([small, cum, jnp.zeros((tok - 2 * srows, tok), F32)], axis=0).T

    row_i = lax.broadcasted_iota(jnp.int32, (size, size), 0)
    col_i = lax.broadcasted_iota(jnp.int32, (size, size), 1)
    time_r = jnp.where(row_i < tok, 2 * row_i, 2 * row_i - 2 * tok + 1)
    time_c = jnp.where(col_i < tok, 2 * col_i, 2 * col_i - 2 * tok + 1)

    for h in range(heads):
        kk = [k_ref[:, j * width + h * DK : j * width + (h + 1) * DK] for j in range(2)]
        keys = jnp.concatenate(kk, axis=0)
        gram = dot_nt(keys, keys)
        cum_col = cols[:, srows + 2 * heads + h : srows + 2 * heads + h + 1]
        cum_row = cum[2 * heads + h : 2 * heads + h + 1, :]
        decay = jnp.where(incl, jnp.exp(jnp.where(incl, cum_col - cum_row, 0.0)), 0.0)
        decay_s = jnp.where(strict, decay, 0.0)
        kf = keys.astype(F32)
        r2 = 1.0 / (jnp.sum(kf * kf, axis=-1, keepdims=True) + 1e-06)
        beta = jnp.concatenate([cols[:, h : h + 1], cols[:, heads + h : heads + h + 1]], axis=0)
        factor = jnp.concatenate(
            [jnp.concatenate([decay_s, decay_s], axis=1), jnp.concatenate([decay, decay_s], axis=1)], axis=0
        )
        a_full = (beta * r2) * factor * gram
        a_sc[h] = a_full
        first = jnp.where((time_r ^ time_c) == 1, a_full, 0.0)
        x0 = jnp.where(time_r == time_c, 1.0, 0.0) - first
        xh_sc[h], xl_sc[h] = split2(x0)

    bit = 1
    while 2 << bit <= size:
        low = time_c >> bit
        picked = ((time_r >> bit) == (low | 1)) & ((low & 1) == 0)
        for h in range(heads):
            b = split2(jnp.where(picked, a_sc[h], 0.0))
            x = (xh_sc[h], xl_sc[h])
            y = split2(mm3(b, x))
            d = split2(mm3(x, y))
            xh_sc[h] = x[0] - d[0]
            xl_sc[h] = x[1] - d[1]
        bit += 1

    for h in range(heads):
        kk = [k_ref[:, j * width + h * DK : j * width + (h + 1) * DK] for j in range(2)]
        vv = [v_ref[:, j * width + h * DV : j * width + (h + 1) * DV] for j in range(2)]
        keys = jnp.concatenate(kk, axis=0)
        vals = jnp.concatenate(vv, axis=0).astype(F32)
        kf = keys.astype(F32)
        ss = jnp.sum(kf * kf, axis=-1, keepdims=True) + 1e-06
        beta = jnp.concatenate([cols[:, h : h + 1], cols[:, heads + h : heads + h + 1]], axis=0)
        cum_col = cols[:, srows + 2 * heads + h : srows + 2 * heads + h + 1]
        cum_row = cum[2 * heads + h : 2 * heads + h + 1, :]
        ecum = jnp.exp(cum_col)
        ecum2 = jnp.concatenate([ecum, ecum], axis=0)
        rhs = jnp.concatenate([(beta * ecum2 / ss) * kf, (beta * lax.rsqrt(ss)) * vals], axis=1)
        wu = mm3((xh_sc[h], xl_sc[h]), split2(rhs))
        q = q_ref[:, h * DK : (h + 1) * DK]
        qf = q.astype(F32)
        rq = lax.rsqrt(jnp.sum(qf * qf, axis=-1, keepdims=True) + 1e-06)
        decay = jnp.where(incl, jnp.exp(jnp.where(incl, cum_col - cum_row, 0.0)), 0.0)
        qmix = jnp.concatenate([decay, decay], axis=1) * (rq * dot_nt(q, keys))
        last = cum_row[:, tok - 1 : tok]
        to_end = jnp.exp(last - cum_row)
        kt = kf.T * jnp.concatenate([to_end, to_end], axis=1)
        both = mm3(split2(jnp.concatenate([qmix, kt], axis=0)), split2(wu))
        reads_ref[h, :, :DK] = (ecum * rq) * qf - both[:tok, :DK]
        reads_ref[h, :, DK:] = both[:tok, DK:]
        elast = jnp.exp(last)
        maps_ref[h, :, :DK] = jnp.where(row_t == col_t, elast, 0.0) - both[tok:, :DK]
        maps_ref[h, :, DK:] = both[tok:, DK:]


def final_kernel(heads, reads_ref, state_ref, gain_ref, w_ref, out_ref):
    parts = []
    for h in range(heads):
        att = reads_ref[h, :, DK:] + mm3(split2(reads_ref[h, :, :DK]), split2(state_ref[h]))
        inv = lax.rsqrt(jnp.mean(att * att, axis=-1, keepdims=True) + 1e-05)
        parts.append((att * inv * gain_ref[:, h * DV : (h + 1) * DV]).astype(BF16))
    out_ref[...] = dot1(jnp.concatenate(parts, axis=1), w_ref[...])


def batch_mm(left_mat, right_mat):
    return jnp.einsum("hij,hjk->hik", left_mat, right_mat, precision=lax.Precision.HIGHEST)


def compose_stack(earlier, later):
    later_trans = later[..., :DK]
    added = jnp.concatenate([jnp.zeros_like(later_trans), later[..., DK:]], axis=-1)
    return batch_mm(later_trans, earlier) + added


def paired_prefix(total_map, identity_map):
    seq_rank = lax.axis_index("seq")
    levels = lax.axis_size("seq").bit_length() - 1
    running = total_map
    before = identity_map
    for bit_pos in range(levels):
        partner = swapped(running, "seq", bit_pos)
        is_upper = seq_rank // 2**bit_pos % 2 == 1
        earlier_part = jnp.where(is_upper, partner, running)
        later_part = jnp.where(is_upper, running, partner)
        shifted = compose_stack(partner, before)
        before = jnp.where(is_upper, shifted, before)
        running = compose_stack(earlier_part, later_part)
    return before


def local_call(queries, keys2, vals2, small, heads):
    tok = queries.shape[0]
    vmem = pl.BlockSpec(memory_space=pltpu.VMEM)
    return pl.pallas_call(
        functools.partial(local_kernel, heads),
        out_shape=[jax.ShapeDtypeStruct((heads, DK, DK + DV), F32), jax.ShapeDtypeStruct((heads, tok, DK + DV), F32)],
        in_specs=[vmem] * 4,
        out_specs=[vmem] * 2,
        scratch_shapes=[
            pltpu.VMEM((heads, 2 * tok, 2 * tok), F32),
            pltpu.VMEM((heads, 2 * tok, 2 * tok), BF16),
            pltpu.VMEM((heads, 2 * tok, 2 * tok), BF16),
        ],
        compiler_params=pltpu.CompilerParams(vmem_limit_bytes=40 << 20),
        name="local_maps",
    )(queries, keys2, vals2, small)


def shards(queries, key_rows, value_rows, strengths, log_gate, keep_flag, norm_gain, out_weight):
    tok = queries.shape[0]
    heads = strengths.shape[0]
    live = keep_flag.astype(F32)[None, :]
    small = jnp.concatenate(
        [strengths[:, 0] * live, strengths[:, 1] * live, log_gate * live, jnp.zeros((heads, tok), F32)], axis=0
    )
    keys2 = key_rows.reshape(tok, -1)
    vals2 = value_rows.reshape(tok, -1)
    maps, reads = local_call(queries, keys2, vals2, small, heads)
    eye_heads = jnp.broadcast_to(jnp.eye(DK, dtype=F32), (heads, DK, DK))
    identity_map = jnp.concatenate([eye_heads, jnp.zeros((heads, DK, DV), F32)], axis=-1)
    state = paired_prefix(maps, identity_map)[..., DK:]
    vmem = pl.BlockSpec(memory_space=pltpu.VMEM)
    partial_out = pl.pallas_call(
        functools.partial(final_kernel, heads),
        out_shape=jax.ShapeDtypeStruct((tok, out_weight.shape[1]), F32),
        in_specs=[vmem] * 4,
        out_specs=vmem,
        compiler_params=pltpu.CompilerParams(vmem_limit_bytes=40 << 20),
        name="read_project",
    )(reads, state, norm_gain[None, :], out_weight)
    projected = lax.psum_scatter(partial_out, "head", scatter_dimension=0, tiled=True)
    return projected.astype(BF16)


def solution(mesh):
    in_specs = (
        P(("groups", "seq"), "head"),
        P(("groups", "seq"), None, "head"),
        P(("groups", "seq"), None, "head"),
        P("head", None, ("groups", "seq")),
        P("head", ("groups", "seq")),
        P(("groups", "seq")),
        P("head"),
        P("head", None),
    )
    out_specs = P(("groups", "seq", "head"), None)
    return jax.shard_map(shards, mesh=mesh, in_specs=in_specs, out_specs=out_specs, check_vma=False)
```

time: 196 us -> 95.1 us (0.49)
  other arithmetic: 94.5 us -> 3.37 us
  matrix products: 30.1 us -> 2.98 us
  waiting for transfers between devices: 46.8 us -> 58.8 us
  Pallas kernels: 0 us -> 10.4 us
  local copies, waits for them, and re-layouts: 8.42 us -> 3.81 us
    another operation x6 -> x0, other arithmetic: 82 us -> none  [the longest x4 80.1 us: block_pieces(): jax.scipy.linalg.solve_triangular(system, both_sides, lower=True, unit_di...]
    dot_general x11 -> x5, matrix products: 17.4 us -> 2.98 us  [batch_mm(): jnp.einsum('hij,hjk->hik', left_mat, right_mat, precision=lax.Precision.H...]
    ppermute x3, waiting for transfers between devices: 36.7 us -> 48.7 us  [swapped(): lax.ppermute(value, axis, [(i, i ^ 1 << bit) for i in range(lax.axis_size...]
    dot_general x7 -> x0, matrix products: 11.6 us -> none  [the longest x1 2.33 us: block_pieces(): jnp.einsum('...tl,...ld->...td', query_mix, wide_w, precision=highest)]
    pallas_call x0 -> x2, Pallas kernels: none -> 10.4 us  [the longest x1 8.69 us: local_call(): pl.pallas_call(functools.partial(local_kernel, heads), out_shape=[jax.Sha...]
    transpose x4 -> x0, other arithmetic: 2.95 us -> none  [the longest x1 1.86 us: shards(): q_unit = q_unit.transpose(1, 0, 2).reshape(head_count, blocks, BLOCK, DK)]
    reduce_sum x3 -> x0, other arithmetic: 2.76 us -> none  [the longest x2 1.67 us: unit_rows(): jnp.sum(values_in * values_in, axis=-1, keepdims=True) + 1e-06]
    unnamed x22 -> x8, local copies, waits for them, and re-layouts: 0.26 us -> 2.87 us
  transfers between devices with their start and end apart: 4 -> 4, of which waited for: 4 -> 4; matrix products, arithmetic and copies ran while one was open for 7% -> 1% of each run, Pallas kernels for 0% -> 0%
where the time goes in v1:
time: 95.1 us; the launch traced here: 93.7 us
  waiting for transfers between devices  58.8 us (62%)
  between operations  13.6 us (14%)
  Pallas kernels  10.4 us (11%)
  local copies, waits for them, and re-layouts  3.81 us (4%)
  other arithmetic  3.37 us (4%)
  matrix products  2.98 us (3%)
    ppermute x3, waiting for transfers between devices, swapped(): lax.ppermute(value, axis, [(i, i ^ 1 << bit) for i in range(lax.axis_size...  48.7 us
    reduce_scatter x1, waiting for transfers between devices, shards(): lax.psum_scatter(partial_out, 'head', scatter_dimension=0, tiled=True)  10.1 us
    pallas_call x1, Pallas kernels, local_call(): pl.pallas_call(functools.partial(local_kernel, heads), out_shape=[jax.Sha...  8.69 us
    dot_general x5, matrix products, batch_mm(): jnp.einsum('hij,hjk->hik', left_mat, right_mat, precision=lax.Precision.H...  2.98 us
    unnamed x8, local copies, waits for them, and re-layouts  2.87 us
  transfers between devices with their start and end apart: 4, of which 4 were waited for; matrix products, arithmetic and copies ran while one was open for 1% of the time, Pallas kernels for 0%

profile of v1, /device:TPU:31, one launch (start us, length us, event | category | flops | bytes accessed | tf_op | source)
XLA Modules:
  0.0 93.7 jit_solution(17168347539938109805)
XLA Ops:
  6.5 0.0 reduce-scatter.2.cloned.1.call-start
  6.5 0.8 fusion.12
  7.3 0.7 convert_element_type.11
  8.0 1.0 %copy.14 = bf16[16,8,2,512]{3,1,2,0:T(8,128)(2,1)S(1)} copy(bf16[16,8,2,512]{3,2,1,0:T(2,128)(2,1)} %bitcast.18) | data formatting | bytes 524288
  8.9 1.0 %copy.13 = bf16[16,8,2,512]{3,1,2,0:T(8,128)(2,1)S(1)} copy(bf16[16,8,2,512]{3,2,1,0:T(2,128)(2,1)} %bitcast.19) | data formatting | bytes 524288
  9.9 0.1 pad.8.clone
  10.0 0.7 broadcast_multiply_fusion.2
  10.7 0.1 maximum_maximum_fusion.small_ref
  10.8 0.0 copy-start.1
  10.8 0.9 copy-done.1
  11.7 8.7 %local_maps.1 = (f32[4,128,256]{2,1,0:T(8,128)S(1)}, f32[4,128,256]{2,1,0:T(8,128)S(1)}) custom-call(bf16[128,512]{1,0:T(8,128)(2,1)S(1)} %copy-done.1, bf16[128,1024]{1,0:T(8,128)(2,1)S(1)} %bitcast.16, bf16[128,1024]{1,0:T(8,128)(2,1)S(1)} %bitcast.15, f32[16,128]{1,0:T(8,128)S(1)} %maximum_maximum_fusion.small_ref), custom_call_target="tpu_custom_call" | custom-call | tf_op jit(solution)/shard_map/local_maps/pallas_call | solution.py:161
  20.4 0.3 collective-permute-start
  20.7 12.5 %collective-permute-done = f32[4,128,256]{2,1,0:T(8,128)S(1)} collective-permute-done((f32[4,128,256]{2,1,0:T(8,128)S(1)}, f32[4,128,256]{2,1,0:T(8,128)S(1)}, u32[]{:S(2)}, u32[]{:S(2)}) %collective-permute-start) | collective-permute-done | bytes 524320 | tf_op jit(solution)/shard_map/ppermute | solution.py:17
  33.2 0.1 broadcast_select_fusion
  33.3 0.6 convolution_add_fusion.2
  33.9 0.3 collective-permute-start.1
  34.2 11.7 %collective-permute-done.1 = f32[4,128,256]{2,1,0:T(8,128)S(1)} collective-permute-done((f32[4,128,256]{2,1,0:T(8,128)S(1)}, f32[4,128,256]{2,1,0:T(8,128)S(1)}, u32[]{:S(2)}, u32[]{:S(2)}) %collective-permute-start.1) | collective-permute-done | bytes 524320 | tf_op jit(solution)/shard_map/ppermute | solution.py:17
  45.9 0.1 broadcast_select_fusion.1
  46.0 0.6 convolution_add_fusion
  46.6 0.2 collective-permute-start.2
  46.8 0.6 convolution_select_fusion
  47.4 0.0 copy-start
  47.4 0.0 copy-start.2
  47.4 0.6 fusion
  48.1 24.5 %collective-permute-done.2 = f32[4,128,256]{2,1,0:T(8,128)S(1)} collective-permute-done((f32[4,128,256]{2,1,0:T(8,128)S(1)}, f32[4,128,256]{2,1,0:T(8,128)S(1)}, u32[]{:S(2)}, u32[]{:S(2)}) %collective-permute-start.2) | collective-permute-done | bytes 524320 | tf_op jit(solution)/shard_map/ppermute | solution.py:17
  72.5 0.6 fusion.5
  73.2 0.0 copy-done
  73.2 0.0 copy-done.2
  73.2 1.7 %read_project.1 = f32[128,2048]{1,0:T(8,128)} custom-call(f32[4,128,256]{2,1,0:T(8,128)S(1)} %get-tuple-element.7.reads_ref, f32[4,128,128]{2,1,0:T(8,128)S(1)} %fusion.3.state_ref, f32[1,512]{1,0:T(1,128)S(1)} %bitcast.17, bf16[512,2048]{1,0:T(8,128)(2,1)S(1)} %copy-done), custom_call_target="tpu_custom_call" | custom-call | tf_op jit(solution)/shard_map/read_project/pallas_call | solution.py:190
  74.9 0.0 reduce-scatter.2.cloned.1.call-update
  74.9 10.1 %reduce-scatter.2.cloned.1.call-done = f32[64,2048]{1,0:T(8,128)} async-done(((f32[128,2048]{1,0:T(8,128)}), f32[64,2048]{1,0:T(8,128)}) %reduce-scatter.2.cloned.1.call-update) | async-done | bytes 524304 | tf_op jit(solution)/shard_map/reduce_scatter | solution.py:198
  85.1 1.8 %convert_element_type.13 = bf16[64,2048]{1,0:T(8,128)(2,1)} convert(f32[64,2048]{1,0:T(8,128)} %reduce-scatter.2.cloned.1.call-done) | non-fusion elementwise | flops 131072 | bytes 786432 | tf_op jit(solution)/shard_map/convert_element_type | solution.py:199
  (8 shorter events, 0.1 us)
Async XLA Ops:
  6.5 78.5 %reduce-scatter.2.cloned.1.call-start = ((), (), s32[]{:S(2)}) async-start(), calls=%async_computation.1 | async-start | bytes 1572864 | tf_op jit(solution)/shard_map/reduce_scatter | solution.py:198
  10.8 0.9 copy-start.1
  20.4 12.8 %collective-permute-start = (f32[4,128,256]{2,1,0:T(8,128)S(1)}, f32[4,128,256]{2,1,0:T(8,128)S(1)}, u32[]{:S(2)}, u32[]{:S(2)}) collective-permute-start(f32[4,128,256]{2,1,0:T(8,128)S(1)} %get-tuple-element.8), channel_id=1, source_target_pairs={{0,2},{2,0},{4,6},{6,4},{8,10},{10,8},{12,14},{14,12},{1,3},{3,1},... | collective-permute-start | bytes 1572872 | tf_op jit(solution)/shard_map/ppermute | solution.py:17
  33.9 11.9 %collective-permute-start.1 = (f32[4,128,256]{2,1,0:T(8,128)S(1)}, f32[4,128,256]{2,1,0:T(8,128)S(1)}, u32[]{:S(2)}, u32[]{:S(2)}) collective-permute-start(f32[4,128,256]{2,1,0:T(8,128)S(1)} %convolution_add_fusion.2), channel_id=1, source_target_pairs={{0,4},{2,6},{4,0},{6,2},{8,12},{10,14},{12,8},{14,10},{1,5},{3,7},... | collective-permute-start | bytes 1572872 | tf_op jit(solution)/shard_map/ppermute | solution.py:17
  46.6 26.0 %collective-permute-start.2 = (f32[4,128,256]{2,1,0:T(8,128)S(1)}, f32[4,128,256]{2,1,0:T(8,128)S(1)}, u32[]{:S(2)}, u32[]{:S(2)}) collective-permute-start(f32[4,128,256]{2,1,0:T(8,128)S(1)} %convolution_add_fusion), channel_id=1, source_target_pairs={{0,8},{2,10},{4,12},{6,14},{8,0},{10,2},{12,4},{14,6},{1,9},{3,11}... | collective-permute-start | bytes 1572872 | tf_op jit(solution)/shard_map/ppermute | solution.py:17
  47.4 25.8 %copy-start = (bf16[512,2048]{1,0:T(8,128)(2,1)S(1)}, bf16[512,2048]{1,0:T(8,128)(2,1)}, u32[]{:S(2)}) copy-start(bf16[512,2048]{1,0:T(8,128)(2,1)} %w_ref.1) | copy-start | bytes 6291460
  47.4 25.8 %copy-start.2 = (f32[512]{0:T(512)S(1)}, f32[512]{0:T(512)}, u32[]{:S(2)}) copy-start(f32[512]{0:T(512)} %param.14) | copy-start | bytes 6148
Sparse Core Ops, SparseCore 0:
  75.0 9.9 reduce-scatter.1

commit v2 on v1

--- a/solution.py
+++ b/solution.py
@@ -9,12 +9,10 @@
 
 DK = 128
 DV = 128
+UNITS = 2
+CHUNKS = 4
 F32 = jnp.float32
 BF16 = jnp.bfloat16
-
-
-def swapped(value, axis, bit):
-    return lax.ppermute(value, axis, [(i, i ^ 1 << bit) for i in range(lax.axis_size(axis))])
 
 
 def split2(x):
@@ -116,43 +114,117 @@
         reads_ref[h, :, :DK] = (ecum * rq) * qf - both[:tok, :DK]
         reads_ref[h, :, DK:] = both[:tok, DK:]
         elast = jnp.exp(last)
-        maps_ref[h, :, :DK] = jnp.where(row_t == col_t, elast, 0.0) - both[tok:, :DK]
-        maps_ref[h, :, DK:] = both[tok:, DK:]
-
-
-def final_kernel(heads, reads_ref, state_ref, gain_ref, w_ref, out_ref):
-    parts = []
-    for h in range(heads):
-        att = reads_ref[h, :, DK:] + mm3(split2(reads_ref[h, :, :DK]), split2(state_ref[h]))
+        maps_ref[h, :, :DK] = jnp.where(row_t == col_t, elast, 0.0) - both[tok:, :DK].T
+        maps_ref[h, :, DK:] = both[tok:, DK:].T
+
+
+def chain_kernel(
+    heads, maps_ref, reads_ref, gain_ref, w_ref, out_ref,
+    sin, sout, th_sc, tl_sc, nrm, part, other, send_sem, recv_sem, xsend, xrecv,
+):
+    n = lax.axis_size("seq")
+    me = lax.axis_index("seq")
+    core = lax.axis_index("head")
+    sibling = 1 - core
+    right = lax.rem(me + 1, n)
+    barrier = pltpu.get_barrier_semaphore()
+
+    def signal(where):
+        pl.semaphore_signal(barrier, inc=1, device_id=where, device_id_type=pl.DeviceIdType.MESH)
+
+    signal({"head": sibling})
+
+    @pl.when(me < n - 1)
+    def _():
+        signal({"seq": right})
+
+    @pl.when(me > 0)
+    def _():
+        signal({"seq": lax.rem(me + n - 1, n)})
+
+    for h in range(heads):
+        th_sc[h], tl_sc[h] = split2(maps_ref[h, :, :DK])
+    inner = (me > 0) & (me < n - 1)
+
+    @pl.when(inner)
+    def _():
+        pl.semaphore_wait(barrier, 3)
+
+    @pl.when(jnp.logical_not(inner))
+    def _():
+        pl.semaphore_wait(barrier, 2)
+
+    rows = DV // UNITS
+
+    def hop(h, u):
+        span = pl.ds(u * rows, rows)
+        return pltpu.make_async_remote_copy(
+            src_ref=sout.at[h, span],
+            dst_ref=sin.at[h, span],
+            send_sem=send_sem.at[h * UNITS + u],
+            recv_sem=recv_sem.at[h * UNITS + u],
+            device_id={"seq": right},
+            device_id_type=pl.DeviceIdType.MESH,
+        )
+
+    for h in range(heads):
+        for u in range(UNITS):
+            lo, hi = u * rows, (u + 1) * rows
+
+            @pl.when(me == 0)
+            def _():
+                sin[h, lo:hi] = jnp.zeros((rows, DK), F32)
+                sout[h, lo:hi] = maps_ref[h, lo:hi, DK:]
+
+            @pl.when(me > 0)
+            def _():
+                hop(h, u).wait_recv()
+                moved = mm3(split2(sin[h, lo:hi]), (th_sc[h], tl_sc[h]))
+                sout[h, lo:hi] = moved + maps_ref[h, lo:hi, DK:]
+
+            @pl.when(me < n - 1)
+            def _():
+                hop(h, u).start()
+
+    for h in range(heads):
+        state = split2(sin[h])
+        reach = split2(reads_ref[h, :, :DK])
+        seen = dot_nt(reach[0], state[0]) + (dot_nt(reach[0], state[1]) + dot_nt(reach[1], state[0]))
+        att = reads_ref[h, :, DK:] + seen
         inv = lax.rsqrt(jnp.mean(att * att, axis=-1, keepdims=True) + 1e-05)
-        parts.append((att * inv * gain_ref[:, h * DV : (h + 1) * DV]).astype(BF16))
-    out_ref[...] = dot1(jnp.concatenate(parts, axis=1), w_ref[...])
-
-
-def batch_mm(left_mat, right_mat):
-    return jnp.einsum("hij,hjk->hik", left_mat, right_mat, precision=lax.Precision.HIGHEST)
-
-
-def compose_stack(earlier, later):
-    later_trans = later[..., :DK]
-    added = jnp.concatenate([jnp.zeros_like(later_trans), later[..., DK:]], axis=-1)
-    return batch_mm(later_trans, earlier) + added
-
-
-def paired_prefix(total_map, identity_map):
-    seq_rank = lax.axis_index("seq")
-    levels = lax.axis_size("seq").bit_length() - 1
-    running = total_map
-    before = identity_map
-    for bit_pos in range(levels):
-        partner = swapped(running, "seq", bit_pos)
-        is_upper = seq_rank // 2**bit_pos % 2 == 1
-        earlier_part = jnp.where(is_upper, partner, running)
-        later_part = jnp.where(is_upper, running, partner)
-        shifted = compose_stack(partner, before)
-        before = jnp.where(is_upper, shifted, before)
-        running = compose_stack(earlier_part, later_part)
-    return before
+        nrm[:, h * DV : (h + 1) * DV] = (att * inv * gain_ref[:, h * DV : (h + 1) * DV]).astype(BF16)
+
+    half = nrm.shape[0] // 2
+    wide = part.shape[-1]
+    chunks = part.shape[0]
+
+    def cross(c):
+        return pltpu.make_async_remote_copy(
+            src_ref=part.at[c],
+            dst_ref=other.at[c],
+            send_sem=xsend.at[c],
+            recv_sem=xrecv.at[c],
+            device_id={"head": sibling},
+            device_id_type=pl.DeviceIdType.MESH,
+        )
+
+    theirs = nrm[pl.ds(pl.multiple_of(sibling * half, half), half), :]
+    for c in range(chunks):
+        part[c] = dot1(theirs, w_ref[:, c * wide : (c + 1) * wide])
+        cross(c).start()
+    mine = nrm[pl.ds(pl.multiple_of(core * half, half), half), :]
+    for c in range(chunks):
+        own = dot1(mine, w_ref[:, c * wide : (c + 1) * wide])
+        cross(c).wait_recv()
+        out_ref[:, c * wide : (c + 1) * wide] = (own + other[c]).astype(BF16)
+    for c in range(chunks):
+        cross(c).wait_send()
+
+    @pl.when(me < n - 1)
+    def _():
+        for h in range(heads):
+            for u in range(UNITS):
+                hop(h, u).wait_send()
 
 
 def local_call(queries, keys2, vals2, small, heads):
@@ -183,20 +255,29 @@
     keys2 = key_rows.reshape(tok, -1)
     vals2 = value_rows.reshape(tok, -1)
     maps, reads = local_call(queries, keys2, vals2, small, heads)
-    eye_heads = jnp.broadcast_to(jnp.eye(DK, dtype=F32), (heads, DK, DK))
-    identity_map = jnp.concatenate([eye_heads, jnp.zeros((heads, DK, DV), F32)], axis=-1)
-    state = paired_prefix(maps, identity_map)[..., DK:]
     vmem = pl.BlockSpec(memory_space=pltpu.VMEM)
-    partial_out = pl.pallas_call(
-        functools.partial(final_kernel, heads),
-        out_shape=jax.ShapeDtypeStruct((tok, out_weight.shape[1]), F32),
+    wide = out_weight.shape[1]
+    return pl.pallas_call(
+        functools.partial(chain_kernel, heads),
+        out_shape=jax.ShapeDtypeStruct((tok // 2, wide), BF16),
         in_specs=[vmem] * 4,
         out_specs=vmem,
-        compiler_params=pltpu.CompilerParams(vmem_limit_bytes=40 << 20),
-        name="read_project",
-    )(reads, state, norm_gain[None, :], out_weight)
-    projected = lax.psum_scatter(partial_out, "head", scatter_dimension=0, tiled=True)
-    return projected.astype(BF16)
+        scratch_shapes=[
+            pltpu.VMEM((heads, DV, DK), F32),
+            pltpu.VMEM((heads, DV, DK), F32),
+            pltpu.VMEM((heads, DK, DK), BF16),
+            pltpu.VMEM((heads, DK, DK), BF16),
+            pltpu.VMEM((tok, heads * DV), BF16),
+            pltpu.VMEM((CHUNKS, tok // 2, wide // CHUNKS), F32),
+            pltpu.VMEM((CHUNKS, tok // 2, wide // CHUNKS), F32),
+            pltpu.SemaphoreType.DMA((heads * UNITS,)),
+            pltpu.SemaphoreType.DMA((heads * UNITS,)),
+            pltpu.SemaphoreType.DMA((CHUNKS,)),
+            pltpu.SemaphoreType.DMA((CHUNKS,)),
+        ],
+        compiler_params=pltpu.CompilerParams(vmem_limit_bytes=40 << 20, collective_id=0, has_side_effects=True),
+        name="chain_project",
+    )(maps, reads, norm_gain[None, :], out_weight)
 
 
 def solution(mesh):

time: 95.1 us -> 46.8 us (0.49); the launches traced: 93.7 us -> 46.5 us
  waiting for transfers between devices: 58.8 us -> 0 us
  Pallas kernels: 10.4 us -> 38.4 us
  between operations: 13.6 us -> 0.05 us
  matrix products: 2.98 us -> 0 us
  local copies, waits for them, and re-layouts: 3.81 us -> 6.68 us
  other arithmetic: 3.37 us -> 1.42 us
    ppermute x3 -> x0, waiting for transfers between devices: 48.7 us -> none  [swapped(): lax.ppermute(value, axis, [(i, i ^ 1 << bit) for i in range(lax.axis_size...]
    pallas_call x1, Pallas kernels: 1.71 us -> 29.6 us  [shards(): pl.pallas_call(functools.partial(chain_kernel, heads), out_shape=jax.Shap...]
    reduce_scatter x1 -> x0, waiting for transfers between devices: 10.1 us -> none  [shards(): lax.psum_scatter(partial_out, 'head', scatter_dimension=0, tiled=True)]
    dot_general x5 -> x0, matrix products: 2.98 us -> none  [batch_mm(): jnp.einsum('hij,hjk->hik', left_mat, right_mat, precision=lax.Precision.H...]
    unnamed x8 -> x9, local copies, waits for them, and re-layouts: 2.87 us -> 5.83 us
    convert_element_type x2 -> x0, other arithmetic: 1.78 us -> none  [the longest x1 1.77 us: shards(): return projected.astype(BF16)]
  transfers between devices with their start and end apart: 4 -> 0, of which waited for: 4 -> 0; matrix products, arithmetic and copies ran while one was open for 1% -> 0% of each run, Pallas kernels for 0% -> 0%
where the time goes in v2:
time: 46.8 us; the launch traced here: 46.5 us
  Pallas kernels  38.4 us (82%)
  local copies, waits for them, and re-layouts  6.68 us (14%)
  other arithmetic  1.42 us (3%)
    pallas_call x1, Pallas kernels, shards(): pl.pallas_call(functools.partial(chain_kernel, heads), out_shape=jax.Shap...  29.6 us
    pallas_call x1, Pallas kernels, local_call(): pl.pallas_call(functools.partial(local_kernel, heads), out_shape=[jax.Sha...  8.79 us
    unnamed x9, local copies, waits for them, and re-layouts  5.83 us

profile of v2, /device:TPU:31, one launch (start us, length us, event | category | flops | bytes accessed | tf_op | source)
XLA Modules:
  0.0 46.5 jit_solution(8006890894649419683)
XLA Ops:
  0.0 0.7 %convert_element_type.3 = f32[128]{0:T(128)S(1)} convert(s32[128]{0:T(128)} %param.13) | non-fusion elementwise | flops 128 | bytes 1024 | tf_op jit(solution)/shard_map/convert_element_type | solution.py:251
  0.7 0.1 pad.3.clone
  0.7 0.8 %fusion = (f32[4,1,128]{2,1,0:T(1,128)S(1)}, f32[4,1,128]{2,1,0:T(1,128)S(1)}) fusion(f32[4,2,128]{2,1,0:T(2,128)} %param.11), kind=kLoop, calls=%fused_computation.4 | loop fusion | bytes 8192 | tf_op jit(solution)/shard_map/slice | solution.py:253
  1.5 0.7 %broadcast_multiply_fusion.2 = (f32[4,128]{1,0:T(4,128)S(1)}, f32[4,128]{1,0:T(4,128)S(1)}, f32[4,128]{1,0:T(4,128)S(1)}) fusion(f32[4,128]{1,0:T(4,128)S(1)} %bitcast.16, f32[128]{0:T(128)S(1)} %convert_element_type.3, f32[4,128]{1,0:T(4,128)S(1)} %bitcast.17, f32[4,128]{1,0:T(4,128)} %param.12), kind=kLoop, calls=%fused_computation.3 | loop fusion | flops 1536 | bytes 12800 | tf_op jit(solution)/shard_map/mul | solution.py:253
  2.2 0.1 maximum_maximum_fusion.small_ref
  2.3 1.0 %copy.13 = bf16[16,8,2,512]{3,1,2,0:T(8,128)(2,1)S(1)} copy(bf16[16,8,2,512]{3,2,1,0:T(2,128)(2,1)} %bitcast.14) | data formatting | bytes 524288
  3.2 1.0 %copy.14 = bf16[16,8,2,512]{3,1,2,0:T(8,128)(2,1)S(1)} copy(bf16[16,8,2,512]{3,2,1,0:T(2,128)(2,1)} %bitcast.15) | data formatting | bytes 524288
  4.2 0.0 copy-start.1
  4.2 0.9 %copy-done.1 = bf16[128,512]{1,0:T(8,128)(2,1)S(1)} copy-done((bf16[128,512]{1,0:T(8,128)(2,1)S(1)}, bf16[128,512]{1,0:T(8,128)(2,1)}, u32[]{:S(2)}) %copy-start.1) | copy-done | bytes 131096
  5.1 8.8 %local_maps.1 = (f32[4,128,256]{2,1,0:T(8,128)S(1)}, f32[4,128,256]{2,1,0:T(8,128)S(1)}) custom-call(bf16[128,512]{1,0:T(8,128)(2,1)S(1)} %copy-done.1, bf16[128,1024]{1,0:T(8,128)(2,1)S(1)} %bitcast.11, bf16[128,1024]{1,0:T(8,128)(2,1)S(1)} %bitcast.12, f32[16,128]{1,0:T(8,128)S(1)} %maximum_maximum_fusion.small_ref), custom_call_target="tpu_custom_call" | custom-call | tf_op jit(solution)/shard_map/local_maps/pallas_call | solution.py:233
  13.9 0.0 copy-start
  14.0 1.6 %copy-done = bf16[512,2048]{1,0:T(8,128)(2,1)S(1)} copy-done((bf16[512,2048]{1,0:T(8,128)(2,1)S(1)}, bf16[512,2048]{1,0:T(8,128)(2,1)}, u32[]{:S(2)}) %copy-start) | copy-done | bytes 2097176
  15.5 0.0 copy-start.2
  15.5 0.7 %copy-done.2 = f32[512]{0:T(512)S(1)} copy-done((f32[512]{0:T(512)S(1)}, f32[512]{0:T(512)}, u32[]{:S(2)}) %copy-start.2) | copy-done | bytes 2072
  16.2 29.6 %chain_project.1 = bf16[64,2048]{1,0:T(8,128)(2,1)S(1)} custom-call(f32[4,128,256]{2,1,0:T(8,128)S(1)} %get-tuple-element.7.maps_ref, f32[4,128,256]{2,1,0:T(8,128)S(1)} %get-tuple-element.8.reads_ref, f32[1,512]{1,0:T(1,128)S(1)} %bitcast.13, bf16[512,2048]{1,0:T(8,128)(2,1)S(1)} %copy-done), custom_call_target="tpu_custom_call" | custom-call | tf_op jit(solution)/shard_map/chain_project/pallas_call | solution.py:260
  45.8 0.7 %copy.16 = bf16[64,2048]{1,0:T(8,128)(2,1)} copy(bf16[64,2048]{1,0:T(8,128)(2,1)S(1)} %chain_project.1) | data formatting | bytes 524288
  (1 shorter events, 0.0 us)
Async XLA Ops:
  4.2 0.9 %copy-start.1 = (bf16[128,512]{1,0:T(8,128)(2,1)S(1)}, bf16[128,512]{1,0:T(8,128)(2,1)}, u32[]{:S(2)}) copy-start(bf16[128,512]{1,0:T(8,128)(2,1)} %q_ref.1) | copy-start | bytes 393220
  13.9 1.6 %copy-start = (bf16[512,2048]{1,0:T(8,128)(2,1)S(1)}, bf16[512,2048]{1,0:T(8,128)(2,1)}, u32[]{:S(2)}) copy-start(bf16[512,2048]{1,0:T(8,128)(2,1)} %w_ref.1) | copy-start | bytes 6291460
  15.5 0.7 %copy-start.2 = (f32[512]{0:T(512)S(1)}, f32[512]{0:T(512)}, u32[]{:S(2)}) copy-start(f32[512]{0:T(512)} %param.14) | copy-start | bytes 6148

commit v3 on v2

--- a/solution.py
+++ b/solution.py
@@ -9,7 +9,7 @@
 
 DK = 128
 DV = 128
-UNITS = 2
+UNITS = 4
 CHUNKS = 4
 F32 = jnp.float32
 BF16 = jnp.bfloat16
@@ -32,8 +32,18 @@
     return lax.dot_general(a, b, (((1,), (1,)), ((), ())), preferred_element_type=F32)
 
 
-def local_kernel(heads, q_ref, k_ref, v_ref, small_ref, maps_ref, reads_ref, a_sc, xh_sc, xl_sc):
+def local_maps(
+    heads, loads, k_ref, v_ref, bias_ref, th_sc, tl_sc, reads_ref,
+    a_sc, xh_sc, xl_sc, small_ref, q_ref, str_ref, log_ref, keep_ref,
+):
     tok = q_ref.shape[0]
+    for load in loads[:3]:
+        load.wait()
+    live = keep_ref[...].astype(F32)
+    small_ref[...] = jnp.zeros_like(small_ref)
+    small_ref[:heads] = str_ref[:, 0, :] * live
+    small_ref[heads : 2 * heads] = str_ref[:, 1, :] * live
+    small_ref[2 * heads : 3 * heads] = log_ref[...] * live
     size = 2 * tok
     width = heads * DK
     row_t = lax.broadcasted_iota(jnp.int32, (tok, tok), 0)
@@ -88,6 +98,7 @@
             xl_sc[h] = x[1] - d[1]
         bit += 1
 
+    loads[3].wait()
     for h in range(heads):
         kk = [k_ref[:, j * width + h * DK : j * width + (h + 1) * DK] for j in range(2)]
         vv = [v_ref[:, j * width + h * DV : j * width + (h + 1) * DV] for j in range(2)]
@@ -114,14 +125,26 @@
         reads_ref[h, :, :DK] = (ecum * rq) * qf - both[:tok, :DK]
         reads_ref[h, :, DK:] = both[:tok, DK:]
         elast = jnp.exp(last)
-        maps_ref[h, :, :DK] = jnp.where(row_t == col_t, elast, 0.0) - both[tok:, :DK].T
-        maps_ref[h, :, DK:] = both[tok:, DK:].T
+        th_sc[h], tl_sc[h] = split2(jnp.where(row_t == col_t, elast, 0.0) - both[tok:, :DK].T)
+        bias_ref[h] = both[tok:, DK:].T
 
 
 def chain_kernel(
-    heads, maps_ref, reads_ref, gain_ref, w_ref, out_ref,
-    sin, sout, th_sc, tl_sc, nrm, part, other, send_sem, recv_sem, xsend, xrecv,
+    heads, q_hbm, k_ref, v_ref, str_hbm, log_hbm, keep_hbm, gain_hbm, w_hbm, out_ref,
+    a_sc, xh_sc, xl_sc, small_ref, q_ref, str_ref, log_ref, keep_ref,
+    gain_ref, w_ref, load_sem, bias_ref, reads_ref, sin, sout, th_sc, tl_sc, nrm, part, other, send_sem, recv_sem, xsend, xrecv,
 ):
+    pairs = (
+        (str_hbm, str_ref),
+        (log_hbm, log_ref),
+        (keep_hbm, keep_ref),
+        (q_hbm, q_ref),
+        (gain_hbm, gain_ref),
+        (w_hbm, w_ref),
+    )
+    loads = [pltpu.make_async_copy(a, b, load_sem.at[i]) for i, (a, b) in enumerate(pairs)]
+    for load in loads:
+        load.start()
     n = lax.axis_size("seq")
     me = lax.axis_index("seq")
     core = lax.axis_index("head")
@@ -142,8 +165,10 @@
     def _():
         signal({"seq": lax.rem(me + n - 1, n)})
 
-    for h in range(heads):
-        th_sc[h], tl_sc[h] = split2(maps_ref[h, :, :DK])
+    local_maps(
+        heads, loads, k_ref, v_ref, bias_ref, th_sc, tl_sc, reads_ref,
+        a_sc, xh_sc, xl_sc, small_ref, q_ref, str_ref, log_ref, keep_ref,
+    )
     inner = (me > 0) & (me < n - 1)
 
     @pl.when(inner)
@@ -167,26 +192,7 @@
             device_id_type=pl.DeviceIdType.MESH,
         )
 
-    for h in range(heads):
-        for u in range(UNITS):
-            lo, hi = u * rows, (u + 1) * rows
-
-            @pl.when(me == 0)
-            def _():
-                sin[h, lo:hi] = jnp.zeros((rows, DK), F32)
-                sout[h, lo:hi] = maps_ref[h, lo:hi, DK:]
-
-            @pl.when(me > 0)
-            def _():
-                hop(h, u).wait_recv()
-                moved = mm3(split2(sin[h, lo:hi]), (th_sc[h], tl_sc[h]))
-                sout[h, lo:hi] = moved + maps_ref[h, lo:hi, DK:]
-
-            @pl.when(me < n - 1)
-            def _():
-                hop(h, u).start()
-
-    for h in range(heads):
+    def read(h):
         state = split2(sin[h])
         reach = split2(reads_ref[h, :, :DK])
         seen = dot_nt(reach[0], state[0]) + (dot_nt(reach[0], state[1]) + dot_nt(reach[1], state[0]))
@@ -194,6 +200,39 @@
         inv = lax.rsqrt(jnp.mean(att * att, axis=-1, keepdims=True) + 1e-05)
         nrm[:, h * DV : (h + 1) * DV] = (att * inv * gain_ref[:, h * DV : (h + 1) * DV]).astype(BF16)
 
+    loads[4].wait()
+    for h in range(heads):
+        for u in range(UNITS):
+            lo, hi = u * rows, (u + 1) * rows
+
+            @pl.when(me == 0)
+            def _():
+                sin[h, lo:hi] = jnp.zeros((rows, DK), F32)
+                sout[h, lo:hi] = bias_ref[h, lo:hi]
+
+            @pl.when(me > 0)
+            def _():
+                hop(h, u).wait_recv()
+
+            @pl.when(inner)
+            def _():
+                moved = mm3(split2(sin[h, lo:hi]), (th_sc[h], tl_sc[h]))
+                sout[h, lo:hi] = moved + bias_ref[h, lo:hi]
+
+            @pl.when(me < n - 1)
+            def _():
+                hop(h, u).start()
+
+        @pl.when(me == n - 1)
+        def _():
+            read(h)
+
+    @pl.when(me < n - 1)
+    def _():
+        for h in range(heads):
+            read(h)
+
+    loads[5].wait()
     half = nrm.shape[0] // 2
     wide = part.shape[-1]
     chunks = part.shape[0]
@@ -227,42 +266,33 @@
                 hop(h, u).wait_send()
 
 
-def local_call(queries, keys2, vals2, small, heads):
+def shards(queries, key_rows, value_rows, strengths, log_gate, keep_flag, norm_gain, out_weight):
     tok = queries.shape[0]
+    heads = strengths.shape[0]
+    keys2 = key_rows.reshape(tok, -1)
+    vals2 = value_rows.reshape(tok, -1)
     vmem = pl.BlockSpec(memory_space=pltpu.VMEM)
+    hbm = pl.BlockSpec(memory_space=pltpu.HBM)
+    wide = out_weight.shape[1]
     return pl.pallas_call(
-        functools.partial(local_kernel, heads),
-        out_shape=[jax.ShapeDtypeStruct((heads, DK, DK + DV), F32), jax.ShapeDtypeStruct((heads, tok, DK + DV), F32)],
-        in_specs=[vmem] * 4,
-        out_specs=[vmem] * 2,
+        functools.partial(chain_kernel, heads),
+        out_shape=jax.ShapeDtypeStruct((tok // 2, wide), BF16),
+        in_specs=[hbm, vmem, vmem, hbm, hbm, hbm, hbm, hbm],
+        out_specs=vmem,
         scratch_shapes=[
             pltpu.VMEM((heads, 2 * tok, 2 * tok), F32),
             pltpu.VMEM((heads, 2 * tok, 2 * tok), BF16),
             pltpu.VMEM((heads, 2 * tok, 2 * tok), BF16),
-        ],
-        compiler_params=pltpu.CompilerParams(vmem_limit_bytes=40 << 20),
-        name="local_maps",
-    )(queries, keys2, vals2, small)
-
-
-def shards(queries, key_rows, value_rows, strengths, log_gate, keep_flag, norm_gain, out_weight):
-    tok = queries.shape[0]
-    heads = strengths.shape[0]
-    live = keep_flag.astype(F32)[None, :]
-    small = jnp.concatenate(
-        [strengths[:, 0] * live, strengths[:, 1] * live, log_gate * live, jnp.zeros((heads, tok), F32)], axis=0
-    )
-    keys2 = key_rows.reshape(tok, -1)
-    vals2 = value_rows.reshape(tok, -1)
-    maps, reads = local_call(queries, keys2, vals2, small, heads)
-    vmem = pl.BlockSpec(memory_space=pltpu.VMEM)
-    wide = out_weight.shape[1]
-    return pl.pallas_call(
-        functools.partial(chain_kernel, heads),
-        out_shape=jax.ShapeDtypeStruct((tok // 2, wide), BF16),
-        in_specs=[vmem] * 4,
-        out_specs=vmem,
-        scratch_shapes=[
+            pltpu.VMEM((4 * heads, tok), F32),
+            pltpu.VMEM(queries.shape, BF16),
+            pltpu.VMEM(strengths.shape, F32),
+            pltpu.VMEM(log_gate.shape, F32),
+            pltpu.VMEM((1, tok), jnp.int32),
+            pltpu.VMEM((1, heads * DV), F32),
+            pltpu.VMEM(out_weight.shape, BF16),
+            pltpu.SemaphoreType.DMA((6,)),
+            pltpu.VMEM((heads, DV, DK), F32),
+            pltpu.VMEM((heads, tok, DK + DV), F32),
             pltpu.VMEM((heads, DV, DK), F32),
             pltpu.VMEM((heads, DV, DK), F32),
             pltpu.VMEM((heads, DK, DK), BF16),
@@ -275,9 +305,9 @@
             pltpu.SemaphoreType.DMA((CHUNKS,)),
             pltpu.SemaphoreType.DMA((CHUNKS,)),
         ],
-        compiler_params=pltpu.CompilerParams(vmem_limit_bytes=40 << 20, collective_id=0, has_side_effects=True),
+        compiler_params=pltpu.CompilerParams(vmem_limit_bytes=62 << 20, collective_id=0, has_side_effects=True),
         name="chain_project",
-    )(maps, reads, norm_gain[None, :], out_weight)
+    )(queries, keys2, vals2, strengths, log_gate, keep_flag[None, :], norm_gain[None, :], out_weight)
 
 
 def solution(mesh):

time: 46.8 us -> 44.2 us (0.944)
  local copies, waits for them, and re-layouts: 6.68 us -> 5.04 us
  other arithmetic: 1.42 us -> 0 us
  Pallas kernels: 38.4 us -> 38.9 us
    pallas_call x1, Pallas kernels: 29.6 us -> 38.9 us  [shards(): pl.pallas_call(functools.partial(chain_kernel, heads), out_shape=jax.Shap...]
    pallas_call x1 -> x0, Pallas kernels: 8.79 us -> none  [local_call(): pl.pallas_call(functools.partial(local_kernel, heads), out_shape=[jax.Sha...]
    unnamed x9 -> x3, local copies, waits for them, and re-layouts: 5.83 us -> 5.04 us
    slice x1 -> x0, local copies, waits for them, and re-layouts: 0.77 us -> none  [shards(): strengths[:, 0] * live]
    mul x1 -> x0, other arithmetic: 0.68 us -> none  [shards(): strengths[:, 0] * live]
    convert_element_type x1 -> x0, other arithmetic: 0.66 us -> none  [shards(): live = keep_flag.astype(F32)[None, :]]
where the time goes in v3:
time: 44.2 us; the launch traced here: 43.9 us
  Pallas kernels  38.9 us (88%)
  local copies, waits for them, and re-layouts  5.04 us (11%)
    pallas_call x1, Pallas kernels, shards(): pl.pallas_call(functools.partial(chain_kernel, heads), out_shape=jax.Shap...  38.9 us
    unnamed x3, local copies, waits for them, and re-layouts  5.04 us

profile of v3, /device:TPU:31, one launch (start us, length us, event | category | flops | bytes accessed | tf_op | source)
XLA Modules:
  0.0 43.9 jit_solution(10548616502451983501)
XLA Ops:
  0.0 1.7 %copy.9 = bf16[16,8,2,512]{3,1,2,0:T(8,128)(2,1)} copy(bf16[16,8,2,512]{3,2,1,0:T(2,128)(2,1)} %bitcast.8) | data formatting | bytes 524288
  1.7 1.7 %copy.10 = bf16[16,8,2,512]{3,1,2,0:T(8,128)(2,1)} copy(bf16[16,8,2,512]{3,2,1,0:T(2,128)(2,1)} %bitcast.9) | data formatting | bytes 524288
  3.4 38.9 %chain_project.1 = bf16[64,2048]{1,0:T(8,128)(2,1)} custom-call(bf16[128,512]{1,0:T(8,128)(2,1)} %q_hbm.1, bf16[128,1024]{1,0:T(8,128)(2,1)} %bitcast.6, bf16[128,1024]{1,0:T(8,128)(2,1)} %bitcast.7, f32[4,2,128]{2,1,0:T(2,128)} %str_hbm.1, f32[4,128]{1,0:T(4,128)} %log_hbm.1, s32[1,128]{1,0:T(1,128)} %bitcast.11, f32[1,512]{1,0:T(1,128)} %bitcast.10, ...), custom_call_target="tpu_custom_call" | custom-call | tf_op jit(solution)/shard_map/chain_project/pallas_call | solution.py:277
  42.3 1.7 %copy.12 = bf16[64,2048]{1,0:T(8,128)(2,1)} copy(bf16[64,2048]{1,0:T(8,128)(2,1)} %chain_project.1) | data formatting | bytes 524288

commit v4 on v3

--- a/solution.py
+++ b/solution.py
@@ -10,6 +10,7 @@
 DK = 128
 DV = 128
 UNITS = 4
+GROUP = 2
 CHUNKS = 4
 F32 = jnp.float32
 BF16 = jnp.bfloat16
@@ -37,7 +38,7 @@
     a_sc, xh_sc, xl_sc, small_ref, q_ref, str_ref, log_ref, keep_ref,
 ):
     tok = q_ref.shape[0]
-    for load in loads[:3]:
+    for load in loads[:4]:
         load.wait()
     live = keep_ref[...].astype(F32)
     small_ref[...] = jnp.zeros_like(small_ref)
@@ -65,68 +66,70 @@
     time_r = jnp.where(row_i < tok, 2 * row_i, 2 * row_i - 2 * tok + 1)
     time_c = jnp.where(col_i < tok, 2 * col_i, 2 * col_i - 2 * tok + 1)
 
-    for h in range(heads):
-        kk = [k_ref[:, j * width + h * DK : j * width + (h + 1) * DK] for j in range(2)]
-        keys = jnp.concatenate(kk, axis=0)
-        gram = dot_nt(keys, keys)
-        cum_col = cols[:, srows + 2 * heads + h : srows + 2 * heads + h + 1]
-        cum_row = cum[2 * heads + h : 2 * heads + h + 1, :]
-        decay = jnp.where(incl, jnp.exp(jnp.where(incl, cum_col - cum_row, 0.0)), 0.0)
-        decay_s = jnp.where(strict, decay, 0.0)
-        kf = keys.astype(F32)
-        r2 = 1.0 / (jnp.sum(kf * kf, axis=-1, keepdims=True) + 1e-06)
-        beta = jnp.concatenate([cols[:, h : h + 1], cols[:, heads + h : heads + h + 1]], axis=0)
-        factor = jnp.concatenate(
-            [jnp.concatenate([decay_s, decay_s], axis=1), jnp.concatenate([decay, decay_s], axis=1)], axis=0
-        )
-        a_full = (beta * r2) * factor * gram
-        a_sc[h] = a_full
-        first = jnp.where((time_r ^ time_c) == 1, a_full, 0.0)
-        x0 = jnp.where(time_r == time_c, 1.0, 0.0) - first
-        xh_sc[h], xl_sc[h] = split2(x0)
-
-    bit = 1
-    while 2 << bit <= size:
-        low = time_c >> bit
-        picked = ((time_r >> bit) == (low | 1)) & ((low & 1) == 0)
-        for h in range(heads):
-            b = split2(jnp.where(picked, a_sc[h], 0.0))
-            x = (xh_sc[h], xl_sc[h])
-            y = split2(mm3(b, x))
-            d = split2(mm3(x, y))
-            xh_sc[h] = x[0] - d[0]
-            xl_sc[h] = x[1] - d[1]
-        bit += 1
-
-    loads[3].wait()
-    for h in range(heads):
-        kk = [k_ref[:, j * width + h * DK : j * width + (h + 1) * DK] for j in range(2)]
-        vv = [v_ref[:, j * width + h * DV : j * width + (h + 1) * DV] for j in range(2)]
-        keys = jnp.concatenate(kk, axis=0)
-        vals = jnp.concatenate(vv, axis=0).astype(F32)
-        kf = keys.astype(F32)
-        ss = jnp.sum(kf * kf, axis=-1, keepdims=True) + 1e-06
-        beta = jnp.concatenate([cols[:, h : h + 1], cols[:, heads + h : heads + h + 1]], axis=0)
-        cum_col = cols[:, srows + 2 * heads + h : srows + 2 * heads + h + 1]
-        cum_row = cum[2 * heads + h : 2 * heads + h + 1, :]
-        ecum = jnp.exp(cum_col)
-        ecum2 = jnp.concatenate([ecum, ecum], axis=0)
-        rhs = jnp.concatenate([(beta * ecum2 / ss) * kf, (beta * lax.rsqrt(ss)) * vals], axis=1)
-        wu = mm3((xh_sc[h], xl_sc[h]), split2(rhs))
-        q = q_ref[:, h * DK : (h + 1) * DK]
-        qf = q.astype(F32)
-        rq = lax.rsqrt(jnp.sum(qf * qf, axis=-1, keepdims=True) + 1e-06)
-        decay = jnp.where(incl, jnp.exp(jnp.where(incl, cum_col - cum_row, 0.0)), 0.0)
-        qmix = jnp.concatenate([decay, decay], axis=1) * (rq * dot_nt(q, keys))
-        last = cum_row[:, tok - 1 : tok]
-        to_end = jnp.exp(last - cum_row)
-        kt = kf.T * jnp.concatenate([to_end, to_end], axis=1)
-        both = mm3(split2(jnp.concatenate([qmix, kt], axis=0)), split2(wu))
-        reads_ref[h, :, :DK] = (ecum * rq) * qf - both[:tok, :DK]
-        reads_ref[h, :, DK:] = both[:tok, DK:]
-        elast = jnp.exp(last)
-        th_sc[h], tl_sc[h] = split2(jnp.where(row_t == col_t, elast, 0.0) - both[tok:, :DK].T)
-        bias_ref[h] = both[tok:, DK:].T
+    def run(group):
+        for h in group:
+            kk = [k_ref[:, j * width + h * DK : j * width + (h + 1) * DK] for j in range(2)]
+            keys = jnp.concatenate(kk, axis=0)
+            gram = dot_nt(keys, keys)
+            cum_col = cols[:, srows + 2 * heads + h : srows + 2 * heads + h + 1]
+            cum_row = cum[2 * heads + h : 2 * heads + h + 1, :]
+            decay = jnp.where(incl, jnp.exp(jnp.where(incl, cum_col - cum_row, 0.0)), 0.0)
+            decay_s = jnp.where(strict, decay, 0.0)
+            kf = keys.astype(F32)
+            r2 = 1.0 / (jnp.sum(kf * kf, axis=-1, keepdims=True) + 1e-06)
+            beta = jnp.concatenate([cols[:, h : h + 1], cols[:, heads + h : heads + h + 1]], axis=0)
+            factor = jnp.concatenate(
+                [jnp.concatenate([decay_s, decay_s], axis=1), jnp.concatenate([decay, decay_s], axis=1)], axis=0
+            )
+            a_full = (beta * r2) * factor * gram
+            a_sc[h] = a_full
+            first = jnp.where((time_r ^ time_c) == 1, a_full, 0.0)
+            x0 = jnp.where(time_r == time_c, 1.0, 0.0) - first
+            xh_sc[h], xl_sc[h] = split2(x0)
+
+        bit = 1
+        while 2 << bit <= size:
+            low = time_c >> bit
+            picked = ((time_r >> bit) == (low | 1)) & ((low & 1) == 0)
+            for h in group:
+                b = split2(jnp.where(picked, a_sc[h], 0.0))
+                x = (xh_sc[h], xl_sc[h])
+                y = split2(mm3(b, x))
+                d = split2(mm3(x, y))
+                xh_sc[h] = x[0] - d[0]
+                xl_sc[h] = x[1] - d[1]
+            bit += 1
+
+        for h in group:
+            kk = [k_ref[:, j * width + h * DK : j * width + (h + 1) * DK] for j in range(2)]
+            vv = [v_ref[:, j * width + h * DV : j * width + (h + 1) * DV] for j in range(2)]
+            keys = jnp.concatenate(kk, axis=0)
+            vals = jnp.concatenate(vv, axis=0).astype(F32)
+            kf = keys.astype(F32)
+            ss = jnp.sum(kf * kf, axis=-1, keepdims=True) + 1e-06
+            beta = jnp.concatenate([cols[:, h : h + 1], cols[:, heads + h : heads + h + 1]], axis=0)
+            cum_col = cols[:, srows + 2 * heads + h : srows + 2 * heads + h + 1]
+            cum_row = cum[2 * heads + h : 2 * heads + h + 1, :]
+            ecum = jnp.exp(cum_col)
+            ecum2 = jnp.concatenate([ecum, ecum], axis=0)
+            rhs = jnp.concatenate([(beta * ecum2 / ss) * kf, (beta * lax.rsqrt(ss)) * vals], axis=1)
+            wu = mm3((xh_sc[h], xl_sc[h]), split2(rhs))
+            q = q_ref[:, h * DK : (h + 1) * DK]
+            qf = q.astype(F32)
+            rq = lax.rsqrt(jnp.sum(qf * qf, axis=-1, keepdims=True) + 1e-06)
+            decay = jnp.where(incl, jnp.exp(jnp.where(incl, cum_col - cum_row, 0.0)), 0.0)
+            qmix = jnp.concatenate([decay, decay], axis=1) * (rq * dot_nt(q, keys))
+            last = cum_row[:, tok - 1 : tok]
+            to_end = jnp.exp(last - cum_row)
+            kt = kf.T * jnp.concatenate([to_end, to_end], axis=1)
+            both = mm3(split2(jnp.concatenate([qmix, kt], axis=0)), split2(wu))
+            reads_ref[h, :, :DK] = (ecum * rq) * qf - both[:tok, :DK]
+            reads_ref[h, :, DK:] = both[:tok, DK:]
+            elast = jnp.exp(last)
+            th_sc[h], tl_sc[h] = split2(jnp.where(row_t == col_t, elast, 0.0) - both[tok:, :DK].T)
+            bias_ref[h] = both[tok:, DK:].T
+
+    return run
 
 
 def chain_kernel(
@@ -165,32 +168,44 @@
     def _():
         signal({"seq": lax.rem(me + n - 1, n)})
 
-    local_maps(
+    run = local_maps(
         heads, loads, k_ref, v_ref, bias_ref, th_sc, tl_sc, reads_ref,
         a_sc, xh_sc, xl_sc, small_ref, q_ref, str_ref, log_ref, keep_ref,
     )
-    inner = (me > 0) & (me < n - 1)
-
-    @pl.when(inner)
-    def _():
-        pl.semaphore_wait(barrier, 3)
-
-    @pl.when(jnp.logical_not(inner))
-    def _():
-        pl.semaphore_wait(barrier, 2)
 
     rows = DV // UNITS
 
-    def hop(h, u):
+    def hop(h, u, src=None):
         span = pl.ds(u * rows, rows)
         return pltpu.make_async_remote_copy(
-            src_ref=sout.at[h, span],
+            src_ref=(sout if src is None else src).at[h, span],
             dst_ref=sin.at[h, span],
             send_sem=send_sem.at[h * UNITS + u],
             recv_sem=recv_sem.at[h * UNITS + u],
             device_id={"seq": right},
             device_id_type=pl.DeviceIdType.MESH,
         )
+
+    inner = (me > 0) & (me < n - 1)
+    for g in range(0, heads, GROUP):
+        group = range(g, min(g + GROUP, heads))
+        run(group)
+        if g == 0:
+
+            @pl.when(inner)
+            def _():
+                pl.semaphore_wait(barrier, 3)
+
+            @pl.when(jnp.logical_not(inner))
+            def _():
+                pl.semaphore_wait(barrier, 2)
+
+        @pl.when(me == 0)
+        def _():
+            for h in group:
+                for u in range(UNITS):
+                    hop(h, u, bias_ref).start()
+                sin[h] = jnp.zeros((DV, DK), F32)
 
     def read(h):
         state = split2(sin[h])
@@ -205,11 +220,6 @@
         for u in range(UNITS):
             lo, hi = u * rows, (u + 1) * rows
 
-            @pl.when(me == 0)
-            def _():
-                sin[h, lo:hi] = jnp.zeros((rows, DK), F32)
-                sout[h, lo:hi] = bias_ref[h, lo:hi]
-
             @pl.when(me > 0)
             def _():
                 hop(h, u).wait_recv()
@@ -219,7 +229,7 @@
                 moved = mm3(split2(sin[h, lo:hi]), (th_sc[h], tl_sc[h]))
                 sout[h, lo:hi] = moved + bias_ref[h, lo:hi]
 
-            @pl.when(me < n - 1)
+            @pl.when(inner)
             def _():
                 hop(h, u).start()
 

time: 44.2 us -> 44.8 us (1.014)
  Pallas kernels: 38.9 us -> 39.5 us
    pallas_call x1, Pallas kernels: 38.9 us -> 39.5 us  [shards(): pl.pallas_call(functools.partial(chain_kernel, heads), out_shape=jax.Shap...]
where the time goes in v4:
time: 44.8 us; the launch traced here: 44.5 us
  Pallas kernels  39.5 us (88%)
  local copies, waits for them, and re-layouts  5.04 us (11%)
    pallas_call x1, Pallas kernels, shards(): pl.pallas_call(functools.partial(chain_kernel, heads), out_shape=jax.Shap...  39.5 us
    unnamed x3, local copies, waits for them, and re-layouts  5.04 us

profile of v4, /device:TPU:31, one launch (start us, length us, event | category | flops | bytes accessed | tf_op | source)
XLA Modules:
  0.0 44.5 jit_solution(6922383279103865662)
XLA Ops:
  0.0 1.7 %copy.9 = bf16[16,8,2,512]{3,1,2,0:T(8,128)(2,1)} copy(bf16[16,8,2,512]{3,2,1,0:T(2,128)(2,1)} %bitcast.8) | data formatting | bytes 524288
  1.7 1.7 %copy.10 = bf16[16,8,2,512]{3,1,2,0:T(8,128)(2,1)} copy(bf16[16,8,2,512]{3,2,1,0:T(2,128)(2,1)} %bitcast.9) | data formatting | bytes 524288
  3.4 39.5 %chain_project.1 = bf16[64,2048]{1,0:T(8,128)(2,1)} custom-call(bf16[128,512]{1,0:T(8,128)(2,1)} %q_hbm.1, bf16[128,1024]{1,0:T(8,128)(2,1)} %bitcast.6, bf16[128,1024]{1,0:T(8,128)(2,1)} %bitcast.7, f32[4,2,128]{2,1,0:T(2,128)} %str_hbm.1, f32[4,128]{1,0:T(4,128)} %log_hbm.1, s32[1,128]{1,0:T(1,128)} %bitcast.11, f32[1,512]{1,0:T(1,128)} %bitcast.10, ...), custom_call_target="tpu_custom_call" | custom-call | tf_op jit(solution)/shard_map/chain_project/pallas_call | solution.py:287
  42.9 1.7 %copy.12 = bf16[64,2048]{1,0:T(8,128)(2,1)} copy(bf16[64,2048]{1,0:T(8,128)(2,1)} %chain_project.1) | data formatting | bytes 524288

commit v5 on v3

--- a/solution.py
+++ b/solution.py
@@ -130,7 +130,8 @@
 
 
 def chain_kernel(
-    heads, q_hbm, k_ref, v_ref, str_hbm, log_hbm, keep_hbm, gain_hbm, w_hbm, out_ref,
+    heads, q_hbm, k_hbm, v_hbm, str_hbm, log_hbm, keep_hbm, gain_hbm, w_hbm, out_ref,
+    k_raw, v_raw, k_ref, v_ref,
     a_sc, xh_sc, xl_sc, small_ref, q_ref, str_ref, log_ref, keep_ref,
     gain_ref, w_ref, load_sem, bias_ref, reads_ref, sin, sout, th_sc, tl_sc, nrm, part, other, send_sem, recv_sem, xsend, xrecv,
 ):
@@ -141,6 +142,8 @@
         (q_hbm, q_ref),
         (gain_hbm, gain_ref),
         (w_hbm, w_ref),
+        (k_hbm, k_raw),
+        (v_hbm, v_raw),
     )
     loads = [pltpu.make_async_copy(a, b, load_sem.at[i]) for i, (a, b) in enumerate(pairs)]
     for load in loads:
@@ -165,6 +168,9 @@
     def _():
         signal({"seq": lax.rem(me + n - 1, n)})
 
+    for load, raw, flat in ((loads[6], k_raw, k_ref), (loads[7], v_raw, v_ref)):
+        load.wait()
+        flat[...] = raw[...].reshape(flat.shape)
     local_maps(
         heads, loads, k_ref, v_ref, bias_ref, th_sc, tl_sc, reads_ref,
         a_sc, xh_sc, xl_sc, small_ref, q_ref, str_ref, log_ref, keep_ref,
@@ -269,17 +275,19 @@
 def shards(queries, key_rows, value_rows, strengths, log_gate, keep_flag, norm_gain, out_weight):
     tok = queries.shape[0]
     heads = strengths.shape[0]
-    keys2 = key_rows.reshape(tok, -1)
-    vals2 = value_rows.reshape(tok, -1)
     vmem = pl.BlockSpec(memory_space=pltpu.VMEM)
     hbm = pl.BlockSpec(memory_space=pltpu.HBM)
     wide = out_weight.shape[1]
     return pl.pallas_call(
         functools.partial(chain_kernel, heads),
         out_shape=jax.ShapeDtypeStruct((tok // 2, wide), BF16),
-        in_specs=[hbm, vmem, vmem, hbm, hbm, hbm, hbm, hbm],
+        in_specs=[hbm] * 8,
         out_specs=vmem,
         scratch_shapes=[
+            pltpu.VMEM(key_rows.shape, BF16),
+            pltpu.VMEM(value_rows.shape, BF16),
+            pltpu.VMEM((tok, 2 * heads * DK), BF16),
+            pltpu.VMEM((tok, 2 * heads * DV), BF16),
             pltpu.VMEM((heads, 2 * tok, 2 * tok), F32),
             pltpu.VMEM((heads, 2 * tok, 2 * tok), BF16),
             pltpu.VMEM((heads, 2 * tok, 2 * tok), BF16),
@@ -290,7 +298,7 @@
             pltpu.VMEM((1, tok), jnp.int32),
             pltpu.VMEM((1, heads * DV), F32),
             pltpu.VMEM(out_weight.shape, BF16),
-            pltpu.SemaphoreType.DMA((6,)),
+            pltpu.SemaphoreType.DMA((8,)),
             pltpu.VMEM((heads, DV, DK), F32),
             pltpu.VMEM((heads, tok, DK + DV), F32),
             pltpu.VMEM((heads, DV, DK), F32),
@@ -307,7 +315,7 @@
         ],
         compiler_params=pltpu.CompilerParams(vmem_limit_bytes=62 << 20, collective_id=0, has_side_effects=True),
         name="chain_project",
-    )(queries, keys2, vals2, strengths, log_gate, keep_flag[None, :], norm_gain[None, :], out_weight)
+    )(queries, key_rows, value_rows, strengths, log_gate, keep_flag[None, :], norm_gain[None, :], out_weight)
 
 
 def solution(mesh):

time: 44.2 us -> 40.9 us (0.925)
  local copies, waits for them, and re-layouts: 5.04 us -> 1.67 us
    unnamed x3 -> x1, local copies, waits for them, and re-layouts: 5.04 us -> 1.67 us
where the time goes in v5:
time: 40.9 us; the launch traced here: 40.7 us
  Pallas kernels  39 us (95%)
  local copies, waits for them, and re-layouts  1.67 us (4%)
    pallas_call x1, Pallas kernels, shards(): pl.pallas_call(functools.partial(chain_kernel, heads), out_shape=jax.Shap...  39 us
    unnamed x1, local copies, waits for them, and re-layouts  1.67 us

profile of v5, /device:TPU:31, one launch (start us, length us, event | category | flops | bytes accessed | tf_op | source)
XLA Modules:
  0.0 40.7 jit_solution(12723884722754585576)
XLA Ops:
  0.0 39.0 %chain_project.1 = bf16[64,2048]{1,0:T(8,128)(2,1)} custom-call(bf16[128,512]{1,0:T(8,128)(2,1)} %q_hbm.1, bf16[128,2,512]{2,1,0:T(2,128)(2,1)} %k_hbm.1, bf16[128,2,512]{2,1,0:T(2,128)(2,1)} %v_hbm.1, f32[4,2,128]{2,1,0:T(2,128)} %str_hbm.1, f32[4,128]{1,0:T(4,128)} %log_hbm.1, s32[1,128]{1,0:T(1,128)} %bitcast.3, f32[1,512]{1,0:T(1,128)} %bitcast.2, ...), custom_call_target="tpu_custom_call" | custom-call | tf_op jit(solution)/shard_map/chain_project/pallas_call | solution.py:281
  39.0 1.7 %copy.10 = bf16[64,2048]{1,0:T(8,128)(2,1)} copy(bf16[64,2048]{1,0:T(8,128)(2,1)} %chain_project.1) | data formatting | bytes 524288
